TPU v7x, 32 devices: a whole 2x2x4 slice. The times are simulated.
32 devices in a mesh: dp: 16 (over z, y, core), expert: 2 (over x).
Axes of the slice: x: 2, y: 2, z: 4, core: 2. Of those that a mesh axis runs over, the one named last changes fastest.
Arguments:
- tokens: bfloat16 [4096, 2048], P(('dp', 'expert')), may hold values from -6 to 6
- cotangent: bfloat16 [4096, 2048], P(('dp', 'expert')), may hold values from -6 to 6
- expert_ids: int32 [4096, 8], P(('dp', 'expert')), may hold values from 0 to 127, as said below
- route_weights: float32 [4096, 8], P(('dp', 'expert')), may hold values from 0.1 to 1
- join_groups: int32 [16], replicated, may hold values from 0 to 1
- w_gate: bfloat16 [2048, 1024], P('dp', 'expert'), may hold values from -0.125 to 0.125
- w_up: bfloat16 [2048, 1024], P('dp', 'expert'), may hold values from -0.125 to 0.125
- w_down: bfloat16 [2048, 1024], P('dp', 'expert'), may hold values from -0.1875 to 0.1875
Outputs:
- mixed: bfloat16 [4096, 2048], P(('dp', 'expert'))
- grad_gate: bfloat16 [2048, 1024], P('dp', 'expert')
- grad_up: bfloat16 [2048, 1024], P('dp', 'expert')
- grad_down: bfloat16 [2048, 1024], P('dp', 'expert')
Inputs may be any that keep to these rules, and one draw needn't show every extreme that they name: `expert_ids`: each row names 8 different experts; the rows of one device name expert 0 at most 16 times, and the rows of some device exactly 16 times.
All inputs are finite; a program needn't handle non-finite values.
Results may differ from a plain program's by a relative error of at most 0.014.
Values may be sent and summed in bfloat16 or wider, within the bound.
A program may use at most 64 MiB of HBM per device.

v0:
```python
import jax
import jax.numpy as jnp
from jax import lax
from jax.sharding import PartitionSpec as P


def per_device(tokens, cotangent, expert_ids, route_weights, join_groups, w_gate, w_up, w_down):
    highest = lax.Precision.HIGHEST
    tok_count = tokens.shape[0]
    slot_count = tok_count // 8
    slice_width = w_gate.shape[1]
    chosen_mask = expert_ids == 0
    routed = jnp.any(chosen_mask, -1)
    weight = jnp.sum(jnp.where(chosen_mask, route_weights, 0.0), -1)
    places = jnp.cumsum(routed.astype(jnp.int32)) - 1
    slot_ids = jnp.arange(slot_count, dtype=jnp.int32)
    chooser = ((places[None, :] == slot_ids[:, None]) & routed[None, :]).astype(jnp.float32)
    chooser_half = chooser.astype(jnp.bfloat16)
    picked_local = jnp.dot(chooser_half, tokens, preferred_element_type=jnp.float32).astype(
        jnp.bfloat16
    )
    picked = lax.all_gather(picked_local, "expert", axis=0, tiled=True)
    gate_acts = jnp.dot(
        picked, lax.all_gather(w_gate, "dp", axis=0, tiled=True), preferred_element_type=jnp.float32
    )
    up_acts = jnp.dot(
        picked, lax.all_gather(w_up, "dp", axis=0, tiled=True), preferred_element_type=jnp.float32
    )
    hidden = (jax.nn.silu(gate_acts) * up_acts).astype(jnp.bfloat16)
    trans_dims = (((1,), (1,)), ((), ()))
    full_down = lax.all_gather(w_down, "dp", axis=0, tiled=True)
    partial_out = lax.dot_general(hidden, full_down, trans_dims, preferred_element_type=jnp.float32)
    out_rows = lax.psum_scatter(
        partial_out.astype(jnp.bfloat16), "expert", scatter_dimension=0, tiled=True
    ).astype(jnp.float32)
    placed = lax.dot_general(
        chooser,
        out_rows,
        (((0,), (0,)), ((), ())),
        precision=highest,
        preferred_element_type=jnp.float32,
    )
    mixed = (placed * weight[:, None]).astype(jnp.bfloat16)
    scaled = cotangent.astype(jnp.float32) * weight[:, None]
    dpicked_local = jnp.dot(
        chooser, scaled, precision=highest, preferred_element_type=jnp.float32
    ).astype(jnp.bfloat16)
    dpicked = lax.all_gather(dpicked_local, "expert", axis=0, tiled=True)
    hidden_grad = jnp.dot(dpicked, full_down, preferred_element_type=jnp.float32)
    sigma_gate = jax.nn.sigmoid(gate_acts)
    dgate = (hidden_grad * up_acts * sigma_gate * (1.0 + gate_acts * (1.0 - sigma_gate))).astype(
        jnp.bfloat16
    )
    dup = (hidden_grad * gate_acts * sigma_gate).astype(jnp.bfloat16)
    group_total = lax.axis_size("dp")
    mine = jnp.arange(group_total, dtype=jnp.int32) == lax.axis_index("dp")
    active = 1.0 - jnp.sum(jnp.where(mine, join_groups, 0)).astype(jnp.float32)
    col_dims = (((0,), (0,)), ((), ()))

    def term_of(left, right):
        return active * lax.dot_general(left, right, col_dims, preferred_element_type=jnp.float32)

    summed = lax.psum_scatter(
        jnp.concatenate(
            [term_of(picked, dgate), term_of(picked, dup), term_of(dpicked, hidden)], axis=1
        ),
        "dp",
        scatter_dimension=0,
        tiled=True,
    )
    grad_gate = summed[:, :slice_width]
    grad_up = summed[:, slice_width : 2 * slice_width]
    grad_down = summed[:, 2 * slice_width :]
    return (
        mixed,
        grad_gate.astype(jnp.bfloat16),
        grad_up.astype(jnp.bfloat16),
        grad_down.astype(jnp.bfloat16),
    )


def solution(mesh):
    in_specs = (
        P(("dp", "expert"), None),
        P(("dp", "expert"), None),
        P(("dp", "expert"), None),
        P(("dp", "expert"), None),
        P(),
        P("dp", "expert"),
        P("dp", "expert"),
        P("dp", "expert"),
    )
    out_specs = (P(("dp", "expert"), None), P("dp", "expert"), P("dp", "expert"), P("dp", "expert"))
    return jax.shard_map(
        per_device, mesh=mesh, in_specs=in_specs, out_specs=out_specs, check_vma=False
    )
```

profile of v0, /device:TPU:0, one launch (start us, length us, event | category | flops | bytes accessed | tf_op | source)
XLA Modules:
  0.0 300.2 jit_solution(16604740441010829208)
XLA Ops:
  7.2 0.0 copy-start
  7.2 0.0 all-gather.4.cloned.1.call-start
  7.2 0.7 all-gather.4.cloned.1.call-update
  7.9 0.0 all-gather.6.cloned.1.call-start
  8.0 0.7 all-gather.6.cloned.1.call-update
  8.7 0.0 all-gather.8.cloned.1.call-start
  8.7 0.7 all-gather.8.cloned.1.call-update
  9.4 0.0 reduce-scatter.3.cloned.1.call-start
  9.5 1.3 fusion.15
  11.4 0.7 select_reduce_fusion
  12.1 0.1 copy.16
  12.3 0.2 reduce-window.8
  12.4 0.1 add_reduce_fusion
  12.5 1.6 convolution_convert_fusion.1
  14.2 5.9 %all_gather.19 = bf16[32,2048]{1,0:T(8,128)(2,1)S(1)} all-gather(bf16[16,2048]{1,0:T(8,128)(2,1)S(1)} %convolution_convert_fusion.1), channel_id=1, replica_groups=mesh['dp'=16,'expert'=2] {'expert'}, dimensions={0}, use_global_device_ids=true | all-gather | bytes 196608 | tf_op jit(solution)/shard_map/all_gather | solution.py:48
  20.0 0.0 copy-done
  20.0 0.2 convolution_convert_fusion.2
  20.2 4.9 %all_gather.15 = bf16[32,2048]{1,0:T(8,128)(2,1)S(1)} all-gather(bf16[16,2048]{1,0:T(8,128)(2,1)S(1)} %convolution_convert_fusion.2), channel_id=1, replica_groups=mesh['dp'=16,'expert'=2] {'expert'}, dimensions={0}, use_global_device_ids=true | all-gather | bytes 196608 | tf_op jit(solution)/shard_map/all_gather | solution.py:22
  25.1 29.2 %all-gather.4.cloned.1.call-done = bf16[2048,512]{1,0:T(8,128)(2,1)} async-done(((bf16[128,512]{1,0:T(8,128)(2,1)}), bf16[2048,512]{1,0:T(8,128)(2,1)}) %all-gather.4.cloned.1.call-update) | async-done | bytes 2097168 | tf_op jit(solution)/shard_map/all_gather | solution.py:24
  54.4 2.0 fusion.19
  56.4 40.3 %all-gather.6.cloned.1.call-done = bf16[2048,512]{1,0:T(8,128)(2,1)} async-done(((bf16[128,512]{1,0:T(8,128)(2,1)}), bf16[2048,512]{1,0:T(8,128)(2,1)}) %all-gather.6.cloned.1.call-update) | async-done | bytes 2097168 | tf_op jit(solution)/shard_map/all_gather | solution.py:27
  96.7 2.0 multiply_convert_fusion.2
  98.8 40.3 %all-gather.8.cloned.1.call-done = bf16[2048,512]{1,0:T(8,128)(2,1)} async-done(((bf16[128,512]{1,0:T(8,128)(2,1)}), bf16[2048,512]{1,0:T(8,128)(2,1)}) %all-gather.8.cloned.1.call-update) | async-done | bytes 2097168 | tf_op jit(solution)/shard_map/all_gather | solution.py:31
  139.1 0.0 copy-start.1
  139.1 3.1 %convolution_convert_fusion = bf16[32,2048]{1,0:T(8,128)(2,1)} fusion(bf16[32,512]{1,0:T(8,128)(2,1)S(1)} %get-tuple-element.17, bf16[2048,512]{1,0:T(8,128)(2,1)} %all-gather.8.cloned.1.call-done), kind=kOutput, calls=%fused_computation.6 | convolution fusion | flops 67174400 | bytes 2260992 | tf_op jit(solution)/shard_map/dot_general | solution.py:32
  142.2 0.0 reduce-scatter.3.cloned.1.call-update
  142.3 0.0 reduce-scatter.5.cloned.1.call-start
  142.3 0.7 convolution_multiply_fusion
  143.1 0.0 copy-done.1
  143.1 0.5 fusion.20
  143.5 0.8 convolution_multiply_fusion.1
  144.3 0.8 convolution_multiply_fusion.2
  145.1 5.4 %pad_maximum_fusion = f32[2048,1536]{0,1:T(8,128)} fusion(f32[2048,512]{0,1:T(8,128)S(1)} %convolution_multiply_fusion, f32[2048,512]{0,1:T(8,128)S(1)} %convolution_multiply_fusion.1, f32[2048,512]{0,1:T(8,128)S(1)} %convolution_multiply_fusion.2), kind=kLoop, calls=%fused_computation | loop fusion | flops 6291456 | bytes 25165824 | tf_op jit(solution)/shard_map/concatenate | solution.py:64
  150.5 0.0 reduce-scatter.5.cloned.1.call-update
  150.5 1.0 reduce-scatter.3.cloned.1.call-done
  151.5 2.0 fusion
  153.5 136.7 %reduce-scatter.5.cloned.1.call-done = f32[128,1536]{0,1:T(8,128)} async-done(((f32[2048,1536]{0,1:T(8,128)}), f32[128,1536]{0,1:T(8,128)}) %reduce-scatter.5.cloned.1.call-update) | async-done | bytes 786448 | tf_op jit(solution)/shard_map/reduce_scatter | solution.py:63
  290.2 1.2 convert.6
  291.4 0.8 copy.19
  292.2 0.8 copy.18
  292.9 0.8 copy.17
  (3 shorter events, 0.1 us)
Async XLA Ops:
  7.2 12.9 %copy-start = (bf16[128,2048]{1,0:T(8,128)(2,1)S(1)}, bf16[128,2048]{1,0:T(8,128)(2,1)}, u32[]{:S(2)}) copy-start(bf16[128,2048]{1,0:T(8,128)(2,1)} %param.8) | copy-start | bytes 1572868
  7.2 47.2 %all-gather.4.cloned.1.call-start = ((), (), s32[]{:S(2)}) async-start(), calls=%async_computation.2 | async-start | bytes 2228224 | tf_op jit(solution)/shard_map/all_gather | solution.py:24
  7.9 88.8 %all-gather.6.cloned.1.call-start = ((), (), s32[]{:S(2)}) async-start(), calls=%async_computation.3 | async-start | bytes 2228224 | tf_op jit(solution)/shard_map/all_gather | solution.py:27
  8.7 130.4 %all-gather.8.cloned.1.call-start = ((), (), s32[]{:S(2)}) async-start(), calls=%async_computation.4 | async-start | bytes 2228224 | tf_op jit(solution)/shard_map/all_gather | solution.py:31
  9.4 142.1 %reduce-scatter.3.cloned.1.call-start = ((), (), s32[]{:S(2)}) async-start(), calls=%async_computation.5 | async-start | bytes 196608 | tf_op jit(solution)/shard_map/reduce_scatter | solution.py:33
  139.1 4.0 %copy-start.1 = (bf16[2048,512]{1,0:T(8,128)(2,1)S(1)}, bf16[2048,512]{1,0:T(8,128)(2,1)}, u32[]{:S(2)}) copy-start(bf16[2048,512]{1,0:T(8,128)(2,1)} %all-gather.8.cloned.1.call-done) | copy-start | bytes 6291460
  142.3 147.9 %reduce-scatter.5.cloned.1.call-start = ((), (), s32[]{:S(2)}) async-start(), calls=%async_computation.6 | async-start | bytes 13369344 | tf_op jit(solution)/shard_map/reduce_scatter | solution.py:63
Sparse Core Ops, SparseCore 0:
  10.2 44.1 all-gather.3
  56.5 40.1 all-gather.5
  98.9 40.1 all-gather.7
  142.4 9.0 reduce-scatter.2
  155.4 134.7 reduce-scatter.4
where the time goes:
time: 301 us; the launch traced here: 300 us
  waiting for transfers between devices  250 us (83%)
  between operations  14.5 us (5%)
  matrix products  13.7 us (5%)
  blocking collectives  10.8 us (4%)
  other arithmetic  8.91 us (3%)
    reduce_scatter x1, waiting for transfers between devices, per_device(): lax.psum_scatter(jnp.concatenate([term_of(picked, dgate), term_of(picked,...  137 us
    all_gather x1, waiting for transfers between devices, per_device(): full_down = lax.all_gather(w_down, 'dp', axis=0, tiled=True)  40.3 us
    all_gather x1, waiting for transfers between devices, per_device(): lax.all_gather(w_up, 'dp', axis=0, tiled=True)  40.3 us
    all_gather x1, waiting for transfers between devices, per_device(): lax.all_gather(w_gate, 'dp', axis=0, tiled=True)  29.2 us
  transfers between devices with their start and end apart: 5, of which 5 were waited for; matrix products, arithmetic and copies ran while one was open for 6% of the time, Pallas kernels for 0%

commit v1 on v0

--- a/solution.py
+++ b/solution.py
@@ -2,6 +2,19 @@
 import jax.numpy as jnp
 from jax import lax
 from jax.sharding import PartitionSpec as P
+
+
+def ring_gather(array, axis, dim):
+    length, index, extent = (lax.axis_size(axis), lax.axis_index(axis), array.shape[dim])
+    right = [(i, (i + 1) % length) for i in range(length)]
+    whole = jnp.zeros((*array.shape[:dim], length * extent, *array.shape[dim + 1 :]), array.dtype)
+    current = array
+    for step in range(length):
+        owner = (index - step) % length
+        whole = lax.dynamic_update_slice_in_dim(whole, current, owner * extent, axis=dim)
+        if step < length - 1:
+            current = lax.ppermute(current, axis, right)
+    return whole
 
 
 def per_device(tokens, cotangent, expert_ids, route_weights, join_groups, w_gate, w_up, w_down):
@@ -20,9 +33,7 @@
         jnp.bfloat16
     )
     picked = lax.all_gather(picked_local, "expert", axis=0, tiled=True)
-    gate_acts = jnp.dot(
-        picked, lax.all_gather(w_gate, "dp", axis=0, tiled=True), preferred_element_type=jnp.float32
-    )
+    gate_acts = jnp.dot(picked, ring_gather(w_gate, "dp", 0), preferred_element_type=jnp.float32)
     up_acts = jnp.dot(
         picked, lax.all_gather(w_up, "dp", axis=0, tiled=True), preferred_element_type=jnp.float32
     )

time: 301 us -> 285 us (0.947)
  waiting for transfers between devices: 250 us -> 234 us
    ppermute x0 -> x15, waiting for transfers between devices: none -> 97.5 us  [ring_gather(): current = lax.ppermute(current, axis, right)]
    all_gather x1, waiting for transfers between devices: 40.3 us -> 0.01 us  [per_device(): lax.all_gather(w_up, 'dp', axis=0, tiled=True)]
    all_gather x1, waiting for transfers between devices: 40.3 us -> 0.03 us  [per_device(): full_down = lax.all_gather(w_down, 'dp', axis=0, tiled=True)]
    all_gather x1 -> x0, waiting for transfers between devices: 29.2 us -> none  [per_device(): lax.all_gather(w_gate, 'dp', axis=0, tiled=True)]
  transfers between devices with their start and end apart: 5 -> 19, of which waited for: 5 -> 16; matrix products, arithmetic and copies ran while one was open for 6% -> 6% of each run, Pallas kernels for 0% -> 0%
where the time goes in v1:
time: 285 us; the launch traced here: 284 us
  waiting for transfers between devices  234 us (82%)
  between operations  14.7 us (5%)
  matrix products  12 us (4%)
  blocking collectives  10.2 us (4%)
  other arithmetic  8.93 us (3%)
  local copies, waits for them, and re-layouts  3.62 us (1%)
    reduce_scatter x1, waiting for transfers between devices, per_device(): lax.psum_scatter(jnp.concatenate([term_of(picked, dgate), term_of(picked,...  135 us
    ppermute x15, waiting for transfers between devices, ring_gather(): current = lax.ppermute(current, axis, right)  97.5 us
  transfers between devices with their start and end apart: 19, of which 16 were waited for; matrix products, arithmetic and copies ran while one was open for 6% of the time, Pallas kernels for 0%

profile of v1, /device:TPU:0, one launch (start us, length us, event | category | flops | bytes accessed | tf_op | source)
XLA Modules:
  0.0 284.5 jit_solution(8584436386957484149)
XLA Ops:
  7.2 0.0 copy-start
  7.2 0.0 all-gather.3.cloned.1.call-start
  7.2 0.7 all-gather.3.cloned.1.call-update
  7.9 0.0 all-gather.5.cloned.1.call-start
  8.0 0.7 all-gather.5.cloned.1.call-update
  8.7 0.0 reduce-scatter.3.cloned.1.call-start
  8.7 0.5 collective-permute-start
  9.3 7.8 %collective-permute-done = bf16[128,512]{1,0:T(8,128)(2,1)S(1)} collective-permute-done((bf16[128,512]{1,0:T(8,128)(2,1)}, bf16[128,512]{1,0:T(8,128)(2,1)S(1)}, u32[]{:S(2)}, u32[]{:S(2)}) %collective-permute-start) | collective-permute-done | bytes 131104 | tf_op jit(solution)/shard_map/ppermute | solution.py:16
  17.1 0.0 collective-permute-start.1
  17.1 7.2 %collective-permute-done.1 = bf16[128,512]{1,0:T(8,128)(2,1)S(1)} collective-permute-done((bf16[128,512]{1,0:T(8,128)(2,1)S(1)}, bf16[128,512]{1,0:T(8,128)(2,1)S(1)}, u32[]{:S(2)}, u32[]{:S(2)}) %collective-permute-start.1) | collective-permute-done | bytes 131104 | tf_op jit(solution)/shard_map/ppermute | solution.py:16
  24.3 0.0 collective-permute-start.2
  24.3 0.7 select_reduce_fusion
  25.0 7.8 %collective-permute-done.2 = bf16[128,512]{1,0:T(8,128)(2,1)S(1)} collective-permute-done((bf16[128,512]{1,0:T(8,128)(2,1)S(1)}, bf16[128,512]{1,0:T(8,128)(2,1)S(1)}, u32[]{:S(2)}, u32[]{:S(2)}) %collective-permute-start.2) | collective-permute-done | bytes 131104 | tf_op jit(solution)/shard_map/ppermute | solution.py:16
  32.8 0.0 collective-permute-start.3
  32.8 0.1 copy.16
  33.0 0.2 reduce-window.8
  33.1 0.1 add_reduce_fusion
  33.2 0.0 copy-start.2
  33.2 6.7 %collective-permute-done.3 = bf16[128,512]{1,0:T(8,128)(2,1)S(1)} collective-permute-done((bf16[128,512]{1,0:T(8,128)(2,1)S(1)}, bf16[128,512]{1,0:T(8,128)(2,1)S(1)}, u32[]{:S(2)}, u32[]{:S(2)}) %collective-permute-start.3) | collective-permute-done | bytes 131104 | tf_op jit(solution)/shard_map/ppermute | solution.py:16
  39.9 0.0 collective-permute-start.4
  39.9 1.6 convolution_convert_fusion.1
  41.5 7.5 %collective-permute-done.4 = bf16[128,512]{1,0:T(8,128)(2,1)S(1)} collective-permute-done((bf16[128,512]{1,0:T(8,128)(2,1)S(1)}, bf16[128,512]{1,0:T(8,128)(2,1)S(1)}, u32[]{:S(2)}, u32[]{:S(2)}) %collective-permute-start.4) | collective-permute-done | bytes 131104 | tf_op jit(solution)/shard_map/ppermute | solution.py:16
  49.0 0.0 collective-permute-start.5
  49.0 0.2 convolution_convert_fusion.2
  49.2 7.0 %collective-permute-done.5 = bf16[128,512]{1,0:T(8,128)(2,1)S(1)} collective-permute-done((bf16[128,512]{1,0:T(8,128)(2,1)S(1)}, bf16[128,512]{1,0:T(8,128)(2,1)S(1)}, u32[]{:S(2)}, u32[]{:S(2)}) %collective-permute-start.5) | collective-permute-done | bytes 131104 | tf_op jit(solution)/shard_map/ppermute | solution.py:16
  56.2 0.0 collective-permute-start.6
  56.2 5.2 %all_gather.15 = bf16[32,2048]{1,0:T(8,128)(2,1)S(1)} all-gather(bf16[16,2048]{1,0:T(8,128)(2,1)S(1)} %convolution_convert_fusion.1), channel_id=1, replica_groups=mesh['dp'=16,'expert'=2] {'expert'}, dimensions={0}, use_global_device_ids=true | all-gather | bytes 196608 | tf_op jit(solution)/shard_map/all_gather | solution.py:59
  61.4 1.3 fusion.15
  62.7 0.5 collective-permute-done.6
  63.3 0.0 collective-permute-start.7
  63.3 4.9 %all_gather.12 = bf16[32,2048]{1,0:T(8,128)(2,1)S(1)} all-gather(bf16[16,2048]{1,0:T(8,128)(2,1)S(1)} %convolution_convert_fusion.2), channel_id=1, replica_groups=mesh['dp'=16,'expert'=2] {'expert'}, dimensions={0}, use_global_device_ids=true | all-gather | bytes 196608 | tf_op jit(solution)/shard_map/all_gather | solution.py:35
  68.9 0.1 broadcast_in_dim.16
  69.1 1.4 collective-permute-done.7
  70.5 0.0 collective-permute-start.8
  70.5 7.4 %collective-permute-done.8 = bf16[128,512]{1,0:T(8,128)(2,1)S(1)} collective-permute-done((bf16[128,512]{1,0:T(8,128)(2,1)S(1)}, bf16[128,512]{1,0:T(8,128)(2,1)S(1)}, u32[]{:S(2)}, u32[]{:S(2)}) %collective-permute-start.8) | collective-permute-done | bytes 131104 | tf_op jit(solution)/shard_map/ppermute | solution.py:16
  78.0 0.0 collective-permute-start.9
  78.0 7.0 %collective-permute-done.9 = bf16[128,512]{1,0:T(8,128)(2,1)S(1)} collective-permute-done((bf16[128,512]{1,0:T(8,128)(2,1)S(1)}, bf16[128,512]{1,0:T(8,128)(2,1)S(1)}, u32[]{:S(2)}, u32[]{:S(2)}) %collective-permute-start.9) | collective-permute-done | bytes 131104 | tf_op jit(solution)/shard_map/ppermute | solution.py:16
  85.0 0.0 collective-permute-start.10
  85.1 8.6 %collective-permute-done.10 = bf16[128,512]{1,0:T(8,128)(2,1)S(1)} collective-permute-done((bf16[128,512]{1,0:T(8,128)(2,1)S(1)}, bf16[128,512]{1,0:T(8,128)(2,1)S(1)}, u32[]{:S(2)}, u32[]{:S(2)}) %collective-permute-start.10) | collective-permute-done | bytes 131104 | tf_op jit(solution)/shard_map/ppermute | solution.py:16
  93.7 7.4 %collective-permute-done.11 = bf16[128,512]{1,0:T(8,128)(2,1)S(1)} collective-permute-done((bf16[128,512]{1,0:T(8,128)(2,1)S(1)}, bf16[128,512]{1,0:T(8,128)(2,1)S(1)}, u32[]{:S(2)}, u32[]{:S(2)}) %collective-permute-start.11) | collective-permute-done | bytes 131104 | tf_op jit(solution)/shard_map/ppermute | solution.py:16
  101.2 7.0 %collective-permute-done.12 = bf16[128,512]{1,0:T(8,128)(2,1)S(1)} collective-permute-done((bf16[128,512]{1,0:T(8,128)(2,1)S(1)}, bf16[128,512]{1,0:T(8,128)(2,1)S(1)}, u32[]{:S(2)}, u32[]{:S(2)}) %collective-permute-start.12) | collective-permute-done | bytes 131104 | tf_op jit(solution)/shard_map/ppermute | solution.py:16
  108.2 7.0 %collective-permute-done.13 = bf16[128,512]{1,0:T(8,128)(2,1)S(1)} collective-permute-done((bf16[128,512]{1,0:T(8,128)(2,1)S(1)}, bf16[128,512]{1,0:T(8,128)(2,1)S(1)}, u32[]{:S(2)}, u32[]{:S(2)}) %collective-permute-start.13) | collective-permute-done | bytes 131104 | tf_op jit(solution)/shard_map/ppermute | solution.py:16
  115.3 0.0 collective-permute-start.14
  115.3 7.0 %collective-permute-done.14 = bf16[128,512]{1,0:T(8,128)(2,1)S(1)} collective-permute-done((bf16[128,512]{1,0:T(8,128)(2,1)S(1)}, bf16[128,512]{1,0:T(8,128)(2,1)S(1)}, u32[]{:S(2)}, u32[]{:S(2)}) %collective-permute-start.14) | collective-permute-done | bytes 131104 | tf_op jit(solution)/shard_map/ppermute | solution.py:16
  122.4 0.5 fusion.19
  122.9 2.0 multiply_convert_fusion.2
  124.9 0.0 all-gather.5.cloned.1.call-done
  124.9 3.0 %convolution_convert_fusion = bf16[32,2048]{1,0:T(8,128)(2,1)} fusion(bf16[32,512]{1,0:T(8,128)(2,1)S(1)} %get-tuple-element.17, bf16[2048,512]{1,0:T(8,128)(2,1)} %all-gather.5.cloned.1.call-done), kind=kOutput, calls=%fused_computation.6 | convolution fusion | flops 67174400 | bytes 2260992 | tf_op jit(solution)/shard_map/dot_general | solution.py:43
  127.9 0.0 reduce-scatter.3.cloned.1.call-update
  127.9 0.0 reduce-scatter.5.cloned.1.call-start
  128.0 0.7 convolution_multiply_fusion
  128.8 0.8 copy-done.1
  129.5 0.4 fusion.20
  130.0 0.8 convolution_multiply_fusion.1
  130.8 0.8 convolution_multiply_fusion.2
  131.5 5.4 %pad_maximum_fusion = f32[2048,1536]{0,1:T(8,128)} fusion(f32[2048,512]{0,1:T(8,128)S(1)} %convolution_multiply_fusion, f32[2048,512]{0,1:T(8,128)S(1)} %convolution_multiply_fusion.1, f32[2048,512]{0,1:T(8,128)S(1)} %convolution_multiply_fusion.2), kind=kLoop, calls=%fused_computation | loop fusion | flops 6291456 | bytes 25165824 | tf_op jit(solution)/shard_map/concatenate | solution.py:75
  137.0 0.0 reduce-scatter.5.cloned.1.call-update
  137.0 0.0 reduce-scatter.3.cloned.1.call-done
  137.0 2.0 fusion
  139.0 135.4 %reduce-scatter.5.cloned.1.call-done = f32[128,1536]{0,1:T(8,128)} async-done(((f32[2048,1536]{0,1:T(8,128)}), f32[128,1536]{0,1:T(8,128)}) %reduce-scatter.5.cloned.1.call-update) | async-done | bytes 786448 | tf_op jit(solution)/shard_map/reduce_scatter | solution.py:74
  274.4 1.2 convert.6
  275.6 0.8 copy.19
  276.4 0.8 copy.18
  277.2 0.8 copy.17
  (26 shorter events, 0.3 us)
Async XLA Ops:
  7.2 41.9 %copy-start = (bf16[128,2048]{1,0:T(8,128)(2,1)S(1)}, bf16[128,2048]{1,0:T(8,128)(2,1)}, u32[]{:S(2)}) copy-start(bf16[128,2048]{1,0:T(8,128)(2,1)} %param.8) | copy-start | bytes 1572868
  7.2 115.7 %all-gather.3.cloned.1.call-start = ((), (), s32[]{:S(2)}) async-start(), calls=%async_computation.2 | async-start | bytes 2228224 | tf_op jit(solution)/shard_map/all_gather | solution.py:38
  7.9 117.0 %all-gather.5.cloned.1.call-start = ((), (), s32[]{:S(2)}) async-start(), calls=%async_computation.3 | async-start | bytes 2228224 | tf_op jit(solution)/shard_map/all_gather | solution.py:42
  8.7 128.4 %reduce-scatter.3.cloned.1.call-start = ((), (), s32[]{:S(2)}) async-start(), calls=%async_computation.4 | async-start | bytes 196608 | tf_op jit(solution)/shard_map/reduce_scatter | solution.py:44
  8.7 8.4 %collective-permute-start = (bf16[128,512]{1,0:T(8,128)(2,1)}, bf16[128,512]{1,0:T(8,128)(2,1)S(1)}, u32[]{:S(2)}, u32[]{:S(2)}) collective-permute-start(bf16[128,512]{1,0:T(8,128)(2,1)} %param.13), channel_id=1, source_target_pairs={{0,2},{2,4},{4,6},{6,8},{8,10},{10,12},{12,14},{14,16},{16,18},{18... | collective-permute-start | bytes 393224 | tf_op jit(solution)/shard_map/ppermute | solution.py:16
  17.1 7.2 %collective-permute-start.1 = (bf16[128,512]{1,0:T(8,128)(2,1)S(1)}, bf16[128,512]{1,0:T(8,128)(2,1)S(1)}, u32[]{:S(2)}, u32[]{:S(2)}) collective-permute-start(bf16[128,512]{1,0:T(8,128)(2,1)S(1)} %collective-permute-done), channel_id=1, source_target_pairs={{0,2},{2,4},{4,6},{6,8},{8,10},{10,12},{12,14},{14,16},{16,18},{18... | collective-permute-start | bytes 393224 | tf_op jit(solution)/shard_map/ppermute | solution.py:16
  24.3 8.6 %collective-permute-start.2 = (bf16[128,512]{1,0:T(8,128)(2,1)S(1)}, bf16[128,512]{1,0:T(8,128)(2,1)S(1)}, u32[]{:S(2)}, u32[]{:S(2)}) collective-permute-start(bf16[128,512]{1,0:T(8,128)(2,1)S(1)} %collective-permute-done.1), channel_id=1, source_target_pairs={{0,2},{2,4},{4,6},{6,8},{8,10},{10,12},{12,14},{14,16},{16,18},{18... | collective-permute-start | bytes 393224 | tf_op jit(solution)/shard_map/ppermute | solution.py:16
  32.8 7.1 %collective-permute-start.3 = (bf16[128,512]{1,0:T(8,128)(2,1)S(1)}, bf16[128,512]{1,0:T(8,128)(2,1)S(1)}, u32[]{:S(2)}, u32[]{:S(2)}) collective-permute-start(bf16[128,512]{1,0:T(8,128)(2,1)S(1)} %collective-permute-done.2), channel_id=1, source_target_pairs={{0,2},{2,4},{4,6},{6,8},{8,10},{10,12},{12,14},{14,16},{16,18},{18... | collective-permute-start | bytes 393224 | tf_op jit(solution)/shard_map/ppermute | solution.py:16
  33.2 35.8 %copy-start.2 = (bf16[128,512]{1,0:T(8,128)(2,1)S(1)}, bf16[128,512]{1,0:T(8,128)(2,1)}, u32[]{:S(2)}) copy-start(bf16[128,512]{1,0:T(8,128)(2,1)} %param.13) | copy-start | bytes 393220
  39.9 9.1 %collective-permute-start.4 = (bf16[128,512]{1,0:T(8,128)(2,1)S(1)}, bf16[128,512]{1,0:T(8,128)(2,1)S(1)}, u32[]{:S(2)}, u32[]{:S(2)}) collective-permute-start(bf16[128,512]{1,0:T(8,128)(2,1)S(1)} %collective-permute-done.3), channel_id=1, source_target_pairs={{0,2},{2,4},{4,6},{6,8},{8,10},{10,12},{12,14},{14,16},{16,18},{18... | collective-permute-start | bytes 393224 | tf_op jit(solution)/shard_map/ppermute | solution.py:16
  49.0 7.1 %collective-permute-start.5 = (bf16[128,512]{1,0:T(8,128)(2,1)S(1)}, bf16[128,512]{1,0:T(8,128)(2,1)S(1)}, u32[]{:S(2)}, u32[]{:S(2)}) collective-permute-start(bf16[128,512]{1,0:T(8,128)(2,1)S(1)} %collective-permute-done.4), channel_id=1, source_target_pairs={{0,2},{2,4},{4,6},{6,8},{8,10},{10,12},{12,14},{14,16},{16,18},{18... | collective-permute-start | bytes 393224 | tf_op jit(solution)/shard_map/ppermute | solution.py:16
  56.2 7.1 %collective-permute-start.6 = (bf16[128,512]{1,0:T(8,128)(2,1)S(1)}, bf16[128,512]{1,0:T(8,128)(2,1)S(1)}, u32[]{:S(2)}, u32[]{:S(2)}) collective-permute-start(bf16[128,512]{1,0:T(8,128)(2,1)S(1)} %collective-permute-done.5), channel_id=1, source_target_pairs={{0,2},{2,4},{4,6},{6,8},{8,10},{10,12},{12,14},{14,16},{16,18},{18... | collective-permute-start | bytes 393224 | tf_op jit(solution)/shard_map/ppermute | solution.py:16
  63.3 7.2 %collective-permute-start.7 = (bf16[128,512]{1,0:T(8,128)(2,1)S(1)}, bf16[128,512]{1,0:T(8,128)(2,1)S(1)}, u32[]{:S(2)}, u32[]{:S(2)}) collective-permute-start(bf16[128,512]{1,0:T(8,128)(2,1)S(1)} %collective-permute-done.6), channel_id=1, source_target_pairs={{0,2},{2,4},{4,6},{6,8},{8,10},{10,12},{12,14},{14,16},{16,18},{18... | collective-permute-start | bytes 393224 | tf_op jit(solution)/shard_map/ppermute | solution.py:16
  70.5 7.5 %collective-permute-start.8 = (bf16[128,512]{1,0:T(8,128)(2,1)S(1)}, bf16[128,512]{1,0:T(8,128)(2,1)S(1)}, u32[]{:S(2)}, u32[]{:S(2)}) collective-permute-start(bf16[128,512]{1,0:T(8,128)(2,1)S(1)} %collective-permute-done.7), channel_id=1, source_target_pairs={{0,2},{2,4},{4,6},{6,8},{8,10},{10,12},{12,14},{14,16},{16,18},{18... | collective-permute-start | bytes 393224 | tf_op jit(solution)/shard_map/ppermute | solution.py:16
  78.0 7.1 %collective-permute-start.9 = (bf16[128,512]{1,0:T(8,128)(2,1)S(1)}, bf16[128,512]{1,0:T(8,128)(2,1)S(1)}, u32[]{:S(2)}, u32[]{:S(2)}) collective-permute-start(bf16[128,512]{1,0:T(8,128)(2,1)S(1)} %collective-permute-done.8), channel_id=1, source_target_pairs={{0,2},{2,4},{4,6},{6,8},{8,10},{10,12},{12,14},{14,16},{16,18},{18... | collective-permute-start | bytes 393224 | tf_op jit(solution)/shard_map/ppermute | solution.py:16
  85.0 8.6 %collective-permute-start.10 = (bf16[128,512]{1,0:T(8,128)(2,1)S(1)}, bf16[128,512]{1,0:T(8,128)(2,1)S(1)}, u32[]{:S(2)}, u32[]{:S(2)}) collective-permute-start(bf16[128,512]{1,0:T(8,128)(2,1)S(1)} %collective-permute-done.9), channel_id=1, source_target_pairs={{0,2},{2,4},{4,6},{6,8},{8,10},{10,12},{12,14},{14,16},{16,18},{18... | collective-permute-start | bytes 393224 | tf_op jit(solution)/shard_map/ppermute | solution.py:16
  93.7 7.4 %collective-permute-start.11 = (bf16[128,512]{1,0:T(8,128)(2,1)S(1)}, bf16[128,512]{1,0:T(8,128)(2,1)S(1)}, u32[]{:S(2)}, u32[]{:S(2)}) collective-permute-start(bf16[128,512]{1,0:T(8,128)(2,1)S(1)} %collective-permute-done.10), channel_id=1, source_target_pairs={{0,2},{2,4},{4,6},{6,8},{8,10},{10,12},{12,14},{14,16},{16,18},{18... | collective-permute-start | bytes 393224 | tf_op jit(solution)/shard_map/ppermute | solution.py:16
  101.1 7.1 %collective-permute-start.12 = (bf16[128,512]{1,0:T(8,128)(2,1)S(1)}, bf16[128,512]{1,0:T(8,128)(2,1)S(1)}, u32[]{:S(2)}, u32[]{:S(2)}) collective-permute-start(bf16[128,512]{1,0:T(8,128)(2,1)S(1)} %collective-permute-done.11), channel_id=1, source_target_pairs={{0,2},{2,4},{4,6},{6,8},{8,10},{10,12},{12,14},{14,16},{16,18},{18... | collective-permute-start | bytes 393224 | tf_op jit(solution)/shard_map/ppermute | solution.py:16
  108.2 7.1 %collective-permute-start.13 = (bf16[128,512]{1,0:T(8,128)(2,1)S(1)}, bf16[128,512]{1,0:T(8,128)(2,1)S(1)}, u32[]{:S(2)}, u32[]{:S(2)}) collective-permute-start(bf16[128,512]{1,0:T(8,128)(2,1)S(1)} %collective-permute-done.12), channel_id=1, source_target_pairs={{0,2},{2,4},{4,6},{6,8},{8,10},{10,12},{12,14},{14,16},{16,18},{18... | collective-permute-start | bytes 393224 | tf_op jit(solution)/shard_map/ppermute | solution.py:16
  115.3 7.1 %collective-permute-start.14 = (bf16[128,512]{1,0:T(8,128)(2,1)S(1)}, bf16[128,512]{1,0:T(8,128)(2,1)S(1)}, u32[]{:S(2)}, u32[]{:S(2)}) collective-permute-start(bf16[128,512]{1,0:T(8,128)(2,1)S(1)} %collective-permute-done.13), channel_id=1, source_target_pairs={{0,2},{2,4},{4,6},{6,8},{8,10},{10,12},{12,14},{14,16},{16,18},{18... | collective-permute-start | bytes 393224 | tf_op jit(solution)/shard_map/ppermute | solution.py:16
  127.9 1.6 copy-start.1
  127.9 146.5 %reduce-scatter.5.cloned.1.call-start = ((), (), s32[]{:S(2)}) async-start(), calls=%async_computation.5 | async-start | bytes 13369344 | tf_op jit(solution)/shard_map/reduce_scatter | solution.py:74
Sparse Core Ops, SparseCore 0:
  10.2 46.2 all-gather.2
  58.6 42.6 all-gather.4
  128.1 7.5 reduce-scatter.2
  139.6 134.7 reduce-scatter.4
